TPU v7x, 256 devices: a whole 4x4x8 slice. The times are simulated.
256 devices in a mesh: dp: 16 (over y_hi, z), mx: 8 (over x, core), my: 2 (over y_lo).
Axes of the slice: x: 4, y: 4 (y_hi: 2, y_lo: 2; y = y_hi * 2 + y_lo), z: 8, core: 2. Of those that a mesh axis runs over, the one named last changes fastest.
Arguments:
- inputs: bfloat16 [4096, 6144], P('dp', 'mx'), may hold values from -300 to 300
- ln_gain: float32 [6144], P('mx'), may hold values from 0.5 to 1.5
- w_qkv: bfloat16 [3, 6144, 4096], P(None, 'mx', 'my'), may hold values from -1 to 1
- qk_gain: float32 [2, 32, 128], P(None, ('my', 'mx')), may hold values from 0 to 8, as said below
- d_out: bfloat16 [4096, 4096], P('dp', ('my', 'mx')), may hold values from -110 to 110
Outputs:
- input_grad: bfloat16 [4096, 6144], P('dp', 'mx')
- w_grad: bfloat16 [3, 6144, 4096], P(None, ('mx', 'dp'), 'my')
- ln_gain_grad: float32 [6144], P('mx')
- qk_gain_grad: float32 [2, 32, 128], P(None, ('my', 'mx'))
Inputs may be any that keep to these rules, and one draw needn't show every extreme that they name: `qk_gain`: positive.
All inputs are finite; a program needn't handle non-finite values.
Results may differ from a plain program's by a relative error of at most 0.015.
The roundings to bfloat16 on the way count: a program that leaves them out, or rounds other values in their place, can miss the bound.
Values may be sent and summed in bfloat16 or wider, within the bound.
A program may use at most 128 MiB of HBM per device.

v0:
```python
import math
import jax
import jax.numpy as jnp
from jax import lax
from jax.sharding import PartitionSpec as P

PATCH = 256
epsilon = 1e-06


def head_norm(values):
    average = jnp.mean(values, axis=-1, keepdims=True)
    spread = jnp.mean(values * values, axis=-1, keepdims=True) - average * average
    inv_scale = lax.rsqrt(spread + epsilon)
    return ((values - average) * inv_scale, inv_scale)


def norm_back(d_normed, normed, inv_scale, gain_row):
    d_hat = d_normed * gain_row
    return inv_scale * (
        d_hat
        - jnp.mean(d_hat, axis=-1, keepdims=True)
        - normed * jnp.mean(d_hat * normed, axis=-1, keepdims=True)
    )


def body(inputs, ln_gain, w_qkv, qk_gain, d_out):
    token_rows = inputs.shape[0]
    width_local = inputs.shape[1]
    width = width_local * lax.axis_size("mx")
    widened = inputs.astype(jnp.float32)
    totals = lax.psum((jnp.sum(widened, axis=1), jnp.sum(widened * widened, axis=1)), "mx")
    average = totals[0][:, None] / width
    spread = totals[1][:, None] / width - average * average
    inv_scale = lax.rsqrt(spread + epsilon)
    normed = (widened - average) * inv_scale
    scaled = (normed * ln_gain[None, :]).astype(jnp.bfloat16)
    local_heads = qk_gain.shape[1]
    head_size = qk_gain.shape[2]
    group_heads = w_qkv.shape[2] // head_size
    weights = w_qkv.reshape(3, width_local, group_heads, head_size)
    projected = lax.psum_scatter(
        jnp.einsum("td,sdhe->hste", scaled, weights, preferred_element_type=jnp.float32),
        "mx",
        scatter_dimension=0,
        tiled=True,
    ).astype(jnp.bfloat16)
    images = token_rows // PATCH
    shaped = projected.reshape(local_heads, 3, images, PATCH, head_size)
    q_hat, q_inv = head_norm(shaped[:, 0].astype(jnp.float32))
    k_hat, k_inv = head_norm(shaped[:, 1].astype(jnp.float32))
    values = shaped[:, 2]
    q_gain = qk_gain[0][:, None, None, :]
    k_gain = qk_gain[1][:, None, None, :]
    q_normed = (q_hat * q_gain).astype(jnp.bfloat16)
    k_normed = (k_hat * k_gain).astype(jnp.bfloat16)
    factor = 1.0 / math.sqrt(head_size)
    scores = (
        jnp.einsum("hipe,hiqe->hipq", q_normed, k_normed, preferred_element_type=jnp.float32)
        * factor
    )
    row_max = jnp.max(scores, axis=-1, keepdims=True)
    exponent = jnp.exp(scores - row_max)
    probabilities = exponent / jnp.sum(exponent, axis=-1, keepdims=True)
    probs_low = probabilities.astype(jnp.bfloat16)
    grad_heads = (
        d_out.reshape(token_rows, local_heads, head_size)
        .transpose(1, 0, 2)
        .reshape(local_heads, images, PATCH, head_size)
    )
    d_values = jnp.einsum(
        "hipq,hipe->hiqe", probs_low, grad_heads, preferred_element_type=jnp.float32
    ).astype(jnp.bfloat16)
    d_probs = jnp.einsum("hipe,hiqe->hipq", grad_heads, values, preferred_element_type=jnp.float32)
    row_delta = jnp.sum(probabilities * d_probs, axis=-1, keepdims=True)
    d_scores = (probabilities * (d_probs - row_delta) * factor).astype(jnp.bfloat16)
    d_qn = jnp.einsum("hipq,hiqe->hipe", d_scores, k_normed, preferred_element_type=jnp.float32)
    d_kn = jnp.einsum("hipq,hipe->hiqe", d_scores, q_normed, preferred_element_type=jnp.float32)
    head_gain_part = jnp.stack(
        [jnp.sum(d_qn * q_hat, axis=(1, 2)), jnp.sum(d_kn * k_hat, axis=(1, 2))]
    )
    d_query = norm_back(d_qn, q_hat, q_inv, q_gain).astype(jnp.bfloat16)
    d_key = norm_back(d_kn, k_hat, k_inv, k_gain).astype(jnp.bfloat16)

    def head_rows(grads):
        return grads.reshape(local_heads, token_rows, head_size)

    block_rows = width_local // lax.axis_size("dp")
    stacked = jnp.stack([head_rows(d_query), head_rows(d_key), head_rows(d_values)], axis=1)
    gathered = lax.all_gather(stacked, "mx", axis=0, tiled=True)
    d_scaled = jnp.einsum("hste,sdhe->td", gathered, weights, preferred_element_type=jnp.float32)
    feature_part = scaled
    w_rows = lax.psum_scatter(
        jnp.einsum(
            "td,hste->dshe", feature_part, gathered, preferred_element_type=jnp.float32
        ).astype(jnp.bfloat16),
        "dp",
        scatter_dimension=0,
        tiled=True,
    ).astype(jnp.float32)
    w_grad = (
        w_rows.reshape(block_rows, 3, group_heads * head_size)
        .transpose(1, 0, 2)
        .astype(jnp.bfloat16)
    )
    gain_row = ln_gain[None, :]
    d_rows = lax.psum(d_scaled.astype(jnp.bfloat16), "my").astype(jnp.float32)
    d_hat = d_rows * gain_row
    stat_sums = lax.psum((jnp.sum(d_hat, axis=1), jnp.sum(d_hat * normed, axis=1)), "mx")
    sum_first = stat_sums[0]
    sum_second = stat_sums[1]
    result_rows = (
        inv_scale * (d_hat - sum_first[:, None] / width - normed * sum_second[:, None] / width)
    ).astype(jnp.bfloat16)
    feature_part = jnp.sum(d_rows * normed, axis=0)
    head_total, feature_total = lax.psum((head_gain_part, feature_part), "dp")
    return (result_rows, w_grad, feature_total, head_total)


def solution(mesh):
    in_specs = (
        P("dp", "mx"),
        P("mx"),
        P(None, "mx", "my"),
        P(None, ("my", "mx"), None),
        P("dp", ("my", "mx")),
    )
    out_specs = (P("dp", "mx"), P(None, ("mx", "dp"), "my"), P("mx"), P(None, ("my", "mx"), None))
    return jax.shard_map(body, mesh=mesh, in_specs=in_specs, out_specs=out_specs, check_vma=False)
```

profile of v0, /device:TPU:2, one launch (start us, length us, event | category | flops | bytes accessed | tf_op | source)
XLA Modules:
  0.0 439.1 jit_solution(7487721284132833700)
XLA Ops:
  7.2 0.0 copy-start
  7.2 0.0 all-gather.2.cloned.1.call-start
  7.2 0.7 slice_bitcast_fusion.3
  7.9 1.2 fusion.44
  9.1 11.7 %all-reduce.3 = (f32[256]{0:T(256)S(1)}, f32[256]{0:T(256)S(1)}) all-reduce(f32[256]{0:T(256)S(1)} %get-tuple-element.18, f32[256]{0:T(256)S(1)} %get-tuple-element.17), channel_id=1, replica_groups=mesh['dp'=16,'mx'=8,'my'=2] {'mx'}, use_global_device_ids=true, to_apply=%region_3.0 | all-reduce | flops 512 | bytes 4096 | tf_op jit(solution)/shard_map/psum | solution.py:32
  20.8 9.2 %fusion.10 = f32[16,3,256,128]{3,2,0,1:T(8,128)} fusion(bf16[256,768]{1,0:T(8,128)(2,1)} %param.5, f32[768]{0:T(1024)} %param.6, f32[256]{0:T(256)S(1)} %get-tuple-element.36, f32[256]{0:T(256)S(1)} %get-tuple-element.35, bf16[3,768,2048]{2,1,0:T(8,128)(2,1)} %param.7), kind=kOutput, calls=%fused_computation.11 | convolution fusion | flops 2416902144 | bytes 16126976 | tf_op jit(solution)/shard_map/td,sdhe->hste/dot_general | solution.py:43
  30.0 0.0 copy-start.5
  30.0 71.0 %all-reduce.8 = bf16[16,3,256,128]{3,2,0,1:T(8,128)(2,1)S(1)} all-reduce(f32[16,3,256,128]{3,2,0,1:T(8,128)} %fusion.10), channel_id=2, replica_groups=mesh['dp'=16,'mx'=8,'my'=2] {'mx'}, use_global_device_ids=true, to_apply=%region_4.0.clone | all-reduce | flops 1572864 | bytes 9437184
  101.0 0.0 copy-done.5
  101.0 0.6 dynamic-slice
  102.3 0.0 copy-start.2
  102.3 0.3 fusion.52
  102.6 0.4 copy-done.2
  103.1 0.0 copy-done
  103.1 0.2 convolution_bitcast_fusion
  103.3 0.0 copy-start.3
  103.3 1.6 fusion.109
  104.9 0.2 fusion.29
  105.2 1.3 fusion.30
  106.5 2.1 fusion.64
  108.6 0.0 copy-done.3
  108.6 0.6 fusion.84
  109.3 0.8 pad_maximum_fusion
  110.1 0.0 all-gather.2.cloned.1.call-update
  110.1 0.0 copy-start.1
  110.1 0.0 copy-start.4
  110.1 0.0 all-reduce.7.cloned.1.call-start
  110.2 33.7 %all-gather.2.cloned.1.call-done = bf16[16,3,256,128]{3,2,0,1:T(8,128)(2,1)} async-done(((bf16[2,3,256,128]{3,2,0,1:T(8,128)(2,1)}), bf16[16,3,256,128]{3,2,0,1:T(8,128)(2,1)}) %all-gather.2.cloned.1.call-update) | async-done | bytes 3145744 | tf_op jit(solution)/shard_map/all_gather | solution.py:90
  143.8 8.0 %fusion.19 = bf16[256,768]{1,0:T(8,128)(2,1)} fusion(bf16[16,3,256,128]{3,2,0,1:T(8,128)(2,1)} %all-gather.2.cloned.1.call-done, bf16[3,768,2048]{2,1,0:T(8,128)(2,1)} %param.7), kind=kOutput, calls=%fused_computation.14 | convolution fusion | flops 2416115712 | bytes 12976128 | tf_op jit(solution)/shard_map/hste,sdhe->td/dot_general | solution.py:91
  151.8 0.0 all-reduce.7.cloned.1.call-update
  151.8 0.2 reduce-scatter.5.cloned.1.call-start
  152.1 0.0 copy-done.1
  152.1 0.0 copy-done.4
  152.1 8.3 %convert_bitcast_fusion = bf16[768,3,16,128]{0,3,1,2:T(8,128)(2,1)} fusion(bf16[16,3,256,128]{3,2,0,1:T(8,128)(2,1)} %all-gather.2.cloned.1.call-done, bf16[256,768]{1,0:T(8,128)(2,1)S(1)} %copy-done.1, f32[768]{0:T(1024)S(1)} %copy-done.4, f32[256]{0:T(256)S(1)} %get-tuple-element.36, f32[256]{0:T(256)S(1)} %get-tuple-element.35), kind=kOutput, calls=%fused_computation.8 | convolution fusion | flops 2421620736 | bytes 12981248 | tf_op jit(solution)/shard_map/td,hste->dshe/dot_general | solution.py:94
  160.4 13.2 %copy.49 = bf16[768,3,16,128]{3,2,1,0:T(8,128)(2,1)} copy(bf16[768,3,16,128]{0,3,1,2:T(8,128)(2,1)} %convert_bitcast_fusion) | data formatting | bytes 18874368 | tf_op jit(solution)/shard_map/convert_element_type | solution.py:96
  173.6 0.0 reduce-scatter.5.cloned.1.call-update
  173.7 16.8 %all-reduce.7.cloned.1.call-done = bf16[256,768]{1,0:T(8,128)(2,1)} async-done(((bf16[256,768]{1,0:T(8,128)(2,1)}), bf16[256,768]{1,0:T(8,128)(2,1)}) %all-reduce.7.cloned.1.call-update) | async-done | bytes 393232 | tf_op jit(solution)/shard_map/psum | solution.py:107
  190.5 1.4 fusion.43
  191.9 11.5 %all-reduce.2 = (f32[256]{0:T(256)S(1)}, f32[256]{0:T(256)S(1)}) all-reduce(f32[256]{0:T(256)S(1)} %get-tuple-element.5, f32[256]{0:T(256)S(1)} %get-tuple-element.10), channel_id=1, replica_groups=mesh['dp'=16,'mx'=8,'my'=2] {'mx'}, use_global_device_ids=true, to_apply=%region_20.0 | all-reduce | flops 512 | bytes 4096 | tf_op jit(solution)/shard_map/psum | solution.py:109
  203.4 43.4 %all-reduce.1 = (f32[768]{0:T(1024)}, f32[2,2,128]{2,1,0:T(2,128)}) all-reduce(f32[768]{0:T(1024)S(1)} %get-tuple-element.4, f32[2,2,128]{2,1,0:T(2,128)S(1)} %pad_maximum_fusion.1), channel_id=1, replica_groups=mesh['dp'=16,'mx'=8,'my'=2] {'dp'}, use_global_device_ids=true, to_apply=%region_23.0 | all-reduce | flops 1280 | bytes 10240 | tf_op jit(solution)/shard_map/psum | solution.py:116
  246.8 2.1 fusion.41
  248.9 181.5 %reduce-scatter.5.cloned.1.call-done = bf16[48,3,16,128]{3,2,1,0:T(8,128)(2,1)} async-done(((bf16[768,3,16,128]{3,2,1,0:T(8,128)(2,1)}), bf16[48,3,16,128]{3,2,1,0:T(8,128)(2,1)}) %reduce-scatter.5.cloned.1.call-update) | async-done | bytes 589840 | tf_op jit(solution)/shard_map/reduce_scatter | solution.py:93
  430.4 1.2 copy.50
  431.6 1.1 convert_element_type.144
  (9 shorter events, 0.1 us)
Async XLA Ops:
  7.2 95.9 %copy-start = (bf16[256,256]{1,0:T(8,128)(2,1)S(1)}, bf16[256,256]{1,0:T(8,128)(2,1)}, u32[]{:S(2)}) copy-start(bf16[256,256]{1,0:T(8,128)(2,1)} %param.9) | copy-start | bytes 393220
  7.2 136.6 %all-gather.2.cloned.1.call-start = ((), (), s32[]{:S(2)}) async-start(), calls=%async_computation.1 | async-start | bytes 3538944 | tf_op jit(solution)/shard_map/all_gather | solution.py:90
  30.0 71.0 %copy-start.5 = (u32[256]{0:T(256)S(1)}, u32[256]{0:T(256)}, u32[]{:S(2)}) copy-start(u32[256]{0:T(256)} %constant.29) | copy-start | bytes 3076
  102.3 0.7 copy-start.2
  103.3 5.3 %copy-start.3 = (bf16[2,3,1,256,128]{4,3,0,2,1:T(8,128)(2,1)S(1)}, bf16[2,3,1,256,128]{4,3,0,2,1:T(8,128)(2,1)}, u32[]{:S(2)}) copy-start(bf16[2,3,1,256,128]{4,3,0,2,1:T(8,128)(2,1)} %copy-done.2) | copy-start | bytes 1179652
  110.1 42.0 %copy-start.1 = (bf16[256,768]{1,0:T(8,128)(2,1)S(1)}, bf16[256,768]{1,0:T(8,128)(2,1)}, u32[]{:S(2)}) copy-start(bf16[256,768]{1,0:T(8,128)(2,1)} %param.5) | copy-start | bytes 1179652
  110.1 42.0 %copy-start.4 = (f32[768]{0:T(1024)S(1)}, f32[768]{0:T(1024)}, u32[]{:S(2)}) copy-start(f32[768]{0:T(1024)} %param.6) | copy-start | bytes 9220
  110.1 80.4 %all-reduce.7.cloned.1.call-start = ((), (), s32[]{:S(2)}) async-start(), calls=%async_computation.2 | async-start | bytes 786432 | tf_op jit(solution)/shard_map/psum | solution.py:107
  151.8 278.5 %reduce-scatter.5.cloned.1.call-start = ((), (), s32[]{:S(2)}) async-start(), calls=%async_computation.3 | async-start | bytes 10027008 | tf_op jit(solution)/shard_map/reduce_scatter | solution.py:93
Sparse Core Ops, SparseCore 0:
  110.2 33.5 all-gather.1
  152.0 38.4 all-reduce.6
  194.7 235.6 reduce-scatter.4
where the time goes:
time: 440 us; the launch traced here: 439 us
  waiting for transfers between devices  232 us (53%)
  blocking collectives  138 us (31%)
  matrix products  31 us (7%)
  local copies, waits for them, and re-layouts  17.3 us (4%)
  between operations  14.6 us (3%)
  other arithmetic  6.45 us (1%)
    reduce_scatter x1, waiting for transfers between devices, body(): lax.psum_scatter(jnp.einsum('td,hste->dshe', feature_part, gathered, pref...  181 us
    unnamed x1, blocking collectives  71 us
    psum x1, blocking collectives, body(): head_total, feature_total = lax.psum((head_gain_part, feature_part), 'dp')  43.4 us
    all_gather x1, waiting for transfers between devices, body(): gathered = lax.all_gather(stacked, 'mx', axis=0, tiled=True)  33.7 us
    psum x1, waiting for transfers between devices, body(): d_rows = lax.psum(d_scaled.astype(jnp.bfloat16), 'my').astype(jnp.float32)  16.8 us
    convert_element_type x1, local copies, waits for them, and re-layouts, body(): w_rows = lax.psum_scatter(jnp.einsum('td,hste->dshe', feature_part, gathe...  13.2 us
    psum x1, blocking collectives, body(): lax.psum((jnp.sum(widened, axis=1), jnp.sum(widened * widened, axis=1)),...  11.7 us
    psum x1, blocking collectives, body(): lax.psum((jnp.sum(d_hat, axis=1), jnp.sum(d_hat * normed, axis=1)), 'mx')  11.5 us
  transfers between devices with their start and end apart: 3, of which 3 were waited for; matrix products, arithmetic and copies ran while one was open for 6% of the time, Pallas kernels for 0%

commit v1 on v0

--- a/solution.py
+++ b/solution.py
@@ -1,3 +1,4 @@
+import functools
 import math
 import jax
 import jax.numpy as jnp
@@ -6,6 +7,30 @@
 
 PATCH = 256
 epsilon = 1e-06
+
+
+def form_levels_all_all(slab_in, mesh_name, dim_k):
+    count_all = lax.axis_size(mesh_name)
+    v_now = range(count_all)
+    u1 = map(lambda t: (t, (t + 1) % count_all), v_now)
+    views = list(u1)
+    v_next = range(count_all)
+    inter = map(lambda t: (t, (t - 1) % count_all), v_next)
+    rows = list(inter)
+    upper, latest = ([slab_in], [slab_in])
+    for _ in range(count_all // 2):
+        known = lax.ppermute(upper[-1], axis_name=mesh_name, perm=views)
+        upper.append(known)
+    for _ in tuple(range((count_all - 1) // 2)):
+        val = lax.ppermute(latest[-1], axis_name=mesh_name, perm=rows)
+        latest.append(val)
+    w2 = jnp.concatenate([*upper[::-1], *latest[1:]], axis=dim_k)
+    left_arr = lax.axis_index(mesh_name)
+    ready = jnp.roll(w2, (left_arr - count_all // 2) * slab_in.shape[dim_k], axis=dim_k)
+    return ready
+
+
+fill_pairs_all = functools.partial(form_levels_all_all, mesh_name="mx", dim_k=0)
 
 
 def head_norm(values):
@@ -87,7 +112,7 @@
 
     block_rows = width_local // lax.axis_size("dp")
     stacked = jnp.stack([head_rows(d_query), head_rows(d_key), head_rows(d_values)], axis=1)
-    gathered = lax.all_gather(stacked, "mx", axis=0, tiled=True)
+    gathered = fill_pairs_all(stacked)
     d_scaled = jnp.einsum("hste,sdhe->td", gathered, weights, preferred_element_type=jnp.float32)
     feature_part = scaled
     w_rows = lax.psum_scatter(

time: 440 us -> 428 us (0.973)
  waiting for transfers between devices: 232 us -> 211 us
  starting transfers between devices: 0.3 us -> 5.97 us
    all_gather x1 -> x0, waiting for transfers between devices: 33.7 us -> none  [body(): gathered = lax.all_gather(stacked, 'mx', axis=0, tiled=True)]
    reduce_scatter x1, waiting for transfers between devices: 181 us -> 155 us  [body(): lax.psum_scatter(jnp.einsum('td,hste->dshe', feature_part, gathered, pref...]
    ppermute x0 -> x7, waiting for transfers between devices: none -> 23.1 us  [the longest x4 23 us: form_levels_all_all(): known = lax.ppermute(upper[-1], axis_name=mesh_name, perm=views)]
    psum x1, waiting for transfers between devices: 16.8 us -> 32.4 us  [body(): d_rows = lax.psum(d_scaled.astype(jnp.bfloat16), 'my').astype(jnp.float32)]
    ppermute x0 -> x7, starting transfers between devices: none -> 5.71 us  [the longest x3 5.68 us: form_levels_all_all(): val = lax.ppermute(latest[-1], axis_name=mesh_name, perm=rows)]
  transfers between devices with their start and end apart: 3 -> 9, of which waited for: 3 -> 7; matrix products, arithmetic and copies ran while one was open for 6% -> 6% of each run, Pallas kernels for 0% -> 0%
where the time goes in v1:
time: 428 us; the launch traced here: 427 us
  waiting for transfers between devices  211 us (49%)
  blocking collectives  138 us (32%)
  matrix products  29.2 us (7%)
  local copies, waits for them, and re-layouts  20.6 us (5%)
  between operations  16.5 us (4%)
  starting transfers between devices  5.97 us (1%)
  other arithmetic  5.82 us (1%)
    reduce_scatter x1, waiting for transfers between devices, body(): lax.psum_scatter(jnp.einsum('td,hste->dshe', feature_part, gathered, pref...  155 us
    unnamed x1, blocking collectives  71 us
    psum x1, blocking collectives, body(): head_total, feature_total = lax.psum((head_gain_part, feature_part), 'dp')  43.3 us
    psum x1, waiting for transfers between devices, body(): d_rows = lax.psum(d_scaled.astype(jnp.bfloat16), 'my').astype(jnp.float32)  32.4 us
    ppermute x4, waiting for transfers between devices, form_levels_all_all(): known = lax.ppermute(upper[-1], axis_name=mesh_name, perm=views)  23 us
    convert_element_type x1, local copies, waits for them, and re-layouts, body(): w_rows = lax.psum_scatter(jnp.einsum('td,hste->dshe', feature_part, gathe...  13.2 us
    psum x1, blocking collectives, body(): lax.psum((jnp.sum(d_hat, axis=1), jnp.sum(d_hat * normed, axis=1)), 'mx')  11.9 us
    psum x1, blocking collectives, body(): lax.psum((jnp.sum(widened, axis=1), jnp.sum(widened * widened, axis=1)),...  11.7 us
  transfers between devices with their start and end apart: 9, of which 7 were waited for; matrix products, arithmetic and copies ran while one was open for 6% of the time, Pallas kernels for 0%

profile of v1, /device:TPU:2, one launch (start us, length us, event | category | flops | bytes accessed | tf_op | source)
XLA Modules:
  0.0 426.9 jit_solution(9874352834875479448)
XLA Ops:
  8.1 0.7 slice_bitcast_fusion.3
  8.8 1.2 fusion.44
  9.9 11.7 %all-reduce.3 = (f32[256]{0:T(256)S(1)}, f32[256]{0:T(256)S(1)}) all-reduce(f32[256]{0:T(256)S(1)} %get-tuple-element.18, f32[256]{0:T(256)S(1)} %get-tuple-element.17), channel_id=1, replica_groups=mesh['dp'=16,'mx'=8,'my'=2] {'mx'}, use_global_device_ids=true, to_apply=%region_3.0 | all-reduce | flops 512 | bytes 4096 | tf_op jit(solution)/shard_map/psum | solution.py:57
  21.6 9.2 %fusion.10 = f32[16,3,256,128]{3,2,0,1:T(8,128)} fusion(bf16[256,768]{1,0:T(8,128)(2,1)} %param.5, f32[768]{0:T(1024)} %param.6, f32[256]{0:T(256)S(1)} %get-tuple-element.36, f32[256]{0:T(256)S(1)} %get-tuple-element.35, bf16[3,768,2048]{2,1,0:T(8,128)(2,1)} %param.7), kind=kOutput, calls=%fused_computation.11 | convolution fusion | flops 2416902144 | bytes 16126976 | tf_op jit(solution)/shard_map/td,sdhe->hste/dot_general | solution.py:68
  30.8 71.0 %all-reduce.8 = bf16[16,3,256,128]{3,2,0,1:T(8,128)(2,1)S(1)} all-reduce(f32[16,3,256,128]{3,2,0,1:T(8,128)} %fusion.10), channel_id=2, replica_groups=mesh['dp'=16,'mx'=8,'my'=2] {'mx'}, use_global_device_ids=true, to_apply=%region_4.0.clone | all-reduce | flops 1572864 | bytes 9437184
  101.9 0.6 dynamic-slice
  103.2 0.3 fusion.52
  103.5 0.4 copy-done.2
  103.9 0.2 convolution_bitcast_fusion
  104.2 1.6 fusion.109
  105.8 0.2 fusion.29
  106.0 1.3 fusion.30
  107.3 1.0 fusion.64
  108.4 0.6 fusion.84
  109.1 7.2 %collective-permute-done = bf16[2,3,256,128]{3,2,0,1:T(8,128)(2,1)S(1)} collective-permute-done((bf16[2,3,256,128]{3,2,0,1:T(8,128)(2,1)S(1)}, bf16[2,3,256,128]{3,2,0,1:T(8,128)(2,1)S(1)}, u32[]{:S(2)}, u32[]{:S(2)}) %collective-permute-start) | collective-permute-done | bytes 393248 | tf_op jit(solution)/shard_map/ppermute | solution.py:22
  116.3 1.7 collective-permute-start.4
  118.0 5.5 %collective-permute-done.1 = bf16[2,3,256,128]{3,2,0,1:T(8,128)(2,1)S(1)} collective-permute-done((bf16[2,3,256,128]{3,2,0,1:T(8,128)(2,1)S(1)}, bf16[2,3,256,128]{3,2,0,1:T(8,128)(2,1)S(1)}, u32[]{:S(2)}, u32[]{:S(2)}) %collective-permute-start.1) | collective-permute-done | bytes 393248 | tf_op jit(solution)/shard_map/ppermute | solution.py:22
  123.5 2.0 collective-permute-start.5
  125.5 5.2 %collective-permute-done.2 = bf16[2,3,256,128]{3,2,0,1:T(8,128)(2,1)S(1)} collective-permute-done((bf16[2,3,256,128]{3,2,0,1:T(8,128)(2,1)S(1)}, bf16[2,3,256,128]{3,2,0,1:T(8,128)(2,1)S(1)}, u32[]{:S(2)}, u32[]{:S(2)}) %collective-permute-start.2) | collective-permute-done | bytes 393248 | tf_op jit(solution)/shard_map/ppermute | solution.py:22
  130.7 0.1 collective-permute-done.5
  130.8 1.9 collective-permute-start.6
  132.7 5.2 %collective-permute-done.3 = bf16[2,3,256,128]{3,2,0,1:T(8,128)(2,1)S(1)} collective-permute-done((bf16[2,3,256,128]{3,2,0,1:T(8,128)(2,1)S(1)}, bf16[2,3,256,128]{3,2,0,1:T(8,128)(2,1)S(1)}, u32[]{:S(2)}, u32[]{:S(2)}) %collective-permute-start.3) | collective-permute-done | bytes 393248 | tf_op jit(solution)/shard_map/ppermute | solution.py:22
  137.9 0.1 constant_dynamic-update-slice_fusion.14
  138.1 0.1 constant_dynamic-update-slice_fusion.12
  138.1 0.1 constant_dynamic-update-slice_fusion.11
  138.2 0.1 constant_dynamic-update-slice_fusion.10
  138.2 0.1 constant_dynamic-update-slice_fusion.9
  138.3 0.1 constant_dynamic-update-slice_fusion.8
  138.4 0.1 constant_dynamic-update-slice_fusion.7
  138.4 0.1 constant_dynamic-update-slice_fusion.6
  138.5 0.1 constant_dynamic-update-slice_fusion.5
  138.6 0.1 constant_dynamic-update-slice_fusion.4
  138.6 0.1 constant_dynamic-update-slice_fusion.3
  138.7 0.1 constant_dynamic-update-slice_fusion.2
  138.7 0.1 constant_dynamic-update-slice_fusion.1
  138.9 2.7 copy-done.4
  141.5 7.3 %fusion.19 = bf16[256,768]{1,0:T(8,128)(2,1)} fusion(bf16[3,768,2048]{2,1,0:T(8,128)(2,1)} %param.7, bf16[32,3,256,128]{3,2,0,1:T(8,128)(2,1)S(1)} %constant_dynamic-update-slice_fusion, s32[]{:T(128)S(6)} %select_n.14), kind=kOutput, calls=%fused_computation.14 | convolution fusion | flops 2416115712 | bytes 12976132 | tf_op jit(solution)/shard_map/hste,sdhe->td/dot_general | solution.py:116
  148.8 0.2 reduce-scatter.5.cloned.1.call-start
  149.1 8.3 %convert_bitcast_fusion = bf16[768,3,16,128]{0,3,1,2:T(8,128)(2,1)} fusion(bf16[256,768]{1,0:T(8,128)(2,1)S(1)} %copy-done.1, f32[768]{0:T(1024)S(1)} %copy-done.5, f32[256]{0:T(256)S(1)} %get-tuple-element.36, f32[256]{0:T(256)S(1)} %get-tuple-element.35, bf16[32,3,256,128]{3,2,0,1:T(8,128)(2,1)} %copy-done.4, s32[]{:T(128)S(6)} %select_n.14), kind=kOutput, calls=%fused_computation.8 | convolution fusion | flops 2421620736 | bytes 12981252 | tf_op jit(solution)/shard_map/td,hste->dshe/dot_general | solution.py:119
  157.4 13.2 %copy.49 = bf16[768,3,16,128]{3,2,1,0:T(8,128)(2,1)} copy(bf16[768,3,16,128]{0,3,1,2:T(8,128)(2,1)} %convert_bitcast_fusion) | data formatting | bytes 18874368 | tf_op jit(solution)/shard_map/convert_element_type | solution.py:121
  170.7 32.4 %all-reduce.7.cloned.1.call-done = bf16[256,768]{1,0:T(8,128)(2,1)} async-done(((bf16[256,768]{1,0:T(8,128)(2,1)}), bf16[256,768]{1,0:T(8,128)(2,1)}) %all-reduce.7.cloned.1.call-update) | async-done | bytes 393232 | tf_op jit(solution)/shard_map/psum | solution.py:132
  203.0 1.5 fusion.43
  204.5 11.9 %all-reduce.2 = (f32[256]{0:T(256)S(1)}, f32[256]{0:T(256)S(1)}) all-reduce(f32[256]{0:T(256)S(1)} %get-tuple-element.5, f32[256]{0:T(256)S(1)} %get-tuple-element.10), channel_id=1, replica_groups=mesh['dp'=16,'mx'=8,'my'=2] {'mx'}, use_global_device_ids=true, to_apply=%region_20.21 | all-reduce | flops 512 | bytes 4096 | tf_op jit(solution)/shard_map/psum | solution.py:134
  216.3 43.3 %all-reduce.1 = (f32[768]{0:T(1024)}, f32[2,2,128]{2,1,0:T(2,128)}) all-reduce(f32[768]{0:T(1024)S(1)} %get-tuple-element.4, f32[2,2,128]{2,1,0:T(2,128)S(1)} %pad_maximum_fusion.1), channel_id=1, replica_groups=mesh['dp'=16,'mx'=8,'my'=2] {'dp'}, use_global_device_ids=true, to_apply=%region_23.24 | all-reduce | flops 1280 | bytes 10240 | tf_op jit(solution)/shard_map/psum | solution.py:141
  259.7 2.1 fusion.41
  261.8 155.5 %reduce-scatter.5.cloned.1.call-done = bf16[48,3,16,128]{3,2,1,0:T(8,128)(2,1)} async-done(((bf16[768,3,16,128]{3,2,1,0:T(8,128)(2,1)}), bf16[48,3,16,128]{3,2,1,0:T(8,128)(2,1)}) %reduce-scatter.5.cloned.1.call-update) | async-done | bytes 589840 | tf_op jit(solution)/shard_map/reduce_scatter | solution.py:118
  417.3 1.2 copy.50
  418.4 1.1 convert_element_type.144
  (34 shorter events, 0.4 us)
Async XLA Ops:
  8.0 95.9 %copy-start = (bf16[256,256]{1,0:T(8,128)(2,1)S(1)}, bf16[256,256]{1,0:T(8,128)(2,1)}, u32[]{:S(2)}) copy-start(bf16[256,256]{1,0:T(8,128)(2,1)} %param.9) | copy-start | bytes 393220
  8.0 195.0 %all-reduce.7.cloned.1.call-start = ((), (), s32[]{:S(2)}) async-start(), calls=%async_computation.1 | async-start | bytes 786432 | tf_op jit(solution)/shard_map/psum | solution.py:132
  30.8 71.0 %copy-start.6 = (u32[256]{0:T(256)S(1)}, u32[256]{0:T(256)}, u32[]{:S(2)}) copy-start(u32[256]{0:T(256)} %constant.62) | copy-start | bytes 3076
  103.2 0.7 copy-start.2
  104.1 3.2 copy-start.3
  109.1 7.2 %collective-permute-start = (bf16[2,3,256,128]{3,2,0,1:T(8,128)(2,1)S(1)}, bf16[2,3,256,128]{3,2,0,1:T(8,128)(2,1)S(1)}, u32[]{:S(2)}, u32[]{:S(2)}) collective-permute-start(bf16[2,3,256,128]{3,2,0,1:T(8,128)(2,1)S(1)} %pad_maximum_fusion), channel_id=1, source_target_pairs={{0,2},{2,4},{4,6},{6,8},{8,10},{10,12},{12,14},{14,0},{1,3},{3,5},... | collective-permute-start | bytes 1179656 | tf_op jit(solution)/shard_map/ppermute | solution.py:22
  116.3 7.2 %collective-permute-start.1 = (bf16[2,3,256,128]{3,2,0,1:T(8,128)(2,1)S(1)}, bf16[2,3,256,128]{3,2,0,1:T(8,128)(2,1)S(1)}, u32[]{:S(2)}, u32[]{:S(2)}) collective-permute-start(bf16[2,3,256,128]{3,2,0,1:T(8,128)(2,1)S(1)} %collective-permute-done), channel_id=1, source_target_pairs={{0,2},{2,4},{4,6},{6,8},{8,10},{10,12},{12,14},{14,0},{1,3},{3,5},... | collective-permute-start | bytes 1179656 | tf_op jit(solution)/shard_map/ppermute | solution.py:22
  116.3 7.2 %collective-permute-start.4 = (bf16[2,3,256,128]{3,2,0,1:T(8,128)(2,1)S(1)}, bf16[2,3,256,128]{3,2,0,1:T(8,128)(2,1)S(1)}, u32[]{:S(2)}, u32[]{:S(2)}) collective-permute-start(bf16[2,3,256,128]{3,2,0,1:T(8,128)(2,1)S(1)} %pad_maximum_fusion), channel_id=1, source_target_pairs={{0,14},{2,0},{4,2},{6,4},{8,6},{10,8},{12,10},{14,12},{1,15},{3,1}... | collective-permute-start | bytes 1179656 | tf_op jit(solution)/shard_map/ppermute | solution.py:25
  123.5 7.2 %collective-permute-start.2 = (bf16[2,3,256,128]{3,2,0,1:T(8,128)(2,1)S(1)}, bf16[2,3,256,128]{3,2,0,1:T(8,128)(2,1)S(1)}, u32[]{:S(2)}, u32[]{:S(2)}) collective-permute-start(bf16[2,3,256,128]{3,2,0,1:T(8,128)(2,1)S(1)} %collective-permute-done.1), channel_id=1, source_target_pairs={{0,2},{2,4},{4,6},{6,8},{8,10},{10,12},{12,14},{14,0},{1,3},{3,5},... | collective-permute-start | bytes 1179656 | tf_op jit(solution)/shard_map/ppermute | solution.py:22
  123.5 7.3 %collective-permute-start.5 = (bf16[2,3,256,128]{3,2,0,1:T(8,128)(2,1)S(1)}, bf16[2,3,256,128]{3,2,0,1:T(8,128)(2,1)S(1)}, u32[]{:S(2)}, u32[]{:S(2)}) collective-permute-start(bf16[2,3,256,128]{3,2,0,1:T(8,128)(2,1)S(1)} %collective-permute-done.4), channel_id=1, source_target_pairs={{0,14},{2,0},{4,2},{6,4},{8,6},{10,8},{12,10},{14,12},{1,15},{3,1}... | collective-permute-start | bytes 1179656 | tf_op jit(solution)/shard_map/ppermute | solution.py:25
  130.7 7.2 %collective-permute-start.3 = (bf16[2,3,256,128]{3,2,0,1:T(8,128)(2,1)S(1)}, bf16[2,3,256,128]{3,2,0,1:T(8,128)(2,1)S(1)}, u32[]{:S(2)}, u32[]{:S(2)}) collective-permute-start(bf16[2,3,256,128]{3,2,0,1:T(8,128)(2,1)S(1)} %collective-permute-done.2), channel_id=1, source_target_pairs={{0,2},{2,4},{4,6},{6,8},{8,10},{10,12},{12,14},{14,0},{1,3},{3,5},... | collective-permute-start | bytes 1179656 | tf_op jit(solution)/shard_map/ppermute | solution.py:22
  130.8 7.5 %collective-permute-start.6 = (bf16[2,3,256,128]{3,2,0,1:T(8,128)(2,1)S(1)}, bf16[2,3,256,128]{3,2,0,1:T(8,128)(2,1)S(1)}, u32[]{:S(2)}, u32[]{:S(2)}) collective-permute-start(bf16[2,3,256,128]{3,2,0,1:T(8,128)(2,1)S(1)} %collective-permute-done.5), channel_id=1, source_target_pairs={{0,14},{2,0},{4,2},{6,4},{8,6},{10,8},{12,10},{14,12},{1,15},{3,1}... | collective-permute-start | bytes 1179656 | tf_op jit(solution)/shard_map/ppermute | solution.py:25
  138.9 2.7 copy-start.4
  141.5 7.5 %copy-start.1 = (bf16[256,768]{1,0:T(8,128)(2,1)S(1)}, bf16[256,768]{1,0:T(8,128)(2,1)}, u32[]{:S(2)}) copy-start(bf16[256,768]{1,0:T(8,128)(2,1)} %param.5) | copy-start | bytes 1179652
  141.5 7.5 %copy-start.5 = (f32[768]{0:T(1024)S(1)}, f32[768]{0:T(1024)}, u32[]{:S(2)}) copy-start(f32[768]{0:T(1024)} %param.6) | copy-start | bytes 9220
  148.8 268.4 %reduce-scatter.5.cloned.1.call-start = ((), (), s32[]{:S(2)}) async-start(), calls=%async_computation.2 | async-start | bytes 10027008 | tf_op jit(solution)/shard_map/reduce_scatter | solution.py:118
Sparse Core Ops, SparseCore 0:
  148.9 54.0 all-reduce.6
Sparse Core Ops, SparseCore 1:
  170.7 246.5 reduce-scatter.4
